TPU v7x, 512 devices: a whole 4x4x16 slice. The times are simulated.
512 devices in a mesh: tile: 32 (over y, x, core), fsdp: 16 (over z).
Axes of the slice: x: 4, y: 4, z: 16, core: 2. Of those that a mesh axis runs over, the one named last changes fastest.
Arguments:
- images: bfloat16 [16, 32, 8, 128, 320], P('fsdp', 'tile'), may hold values from -80 to 80
- tile_rows: int32 [16, 32], P('fsdp', 'tile'), may hold values from 1 to 8, 160 in all within a row
- cotangent: bfloat16 [16, 32, 8, 128, 320], P('fsdp', 'tile'), may hold values from -6 to 6
- master_weight: float32 [2880, 320], P('fsdp'), may hold values from -0.109375 to 0.109375
- norm_gain: float32 [320], replicated, may hold values from 0.5 to 1.5
- norm_bias: float32 [320], replicated, may hold values from -3 to 3
- first_moment: float32 [2880, 320], P('fsdp'), may hold values from -6 to 6
- second_moment: float32 [2880, 320], P('fsdp'), may hold values from 0.5 to 4
Outputs:
- activation: bfloat16 [16, 32, 8, 128, 320], P('fsdp', 'tile')
- image_grad: bfloat16 [16, 32, 8, 128, 320], P('fsdp', 'tile')
- weight_grad: float32 [2880, 320], P('fsdp')
- new_weight: float32 [2880, 320], P('fsdp')
- new_first: float32 [2880, 320], P('fsdp')
- new_second: float32 [2880, 320], P('fsdp')
- gain_grad: float32 [320], replicated
- bias_grad: float32 [320], replicated
Inputs may be any that keep to these rules, and one draw needn't show every extreme that they name: `tile_rows`: in each frame the 32 counts sum to 160 and the largest is exactly 8.
All inputs are finite; a program needn't handle non-finite values. No bound on the sum of `tile_rows` on one device may be relied on, other than what follows from the above.
Results may differ from a plain program's by a relative error of at most 0.027.
Values may be sent and summed in bfloat16 or wider, within the bound.
No kernel may reach another device: no remote copies, remote signals or barrier semaphores. Data moves between devices by JAX's collectives and lax.ppermute only.
A program may use at most 64 MiB of HBM per device.

v0:
```python
import jax
import jax.numpy as jnp
from jax import lax
from jax.sharding import PartitionSpec as P

GROUPS = 32
ROWS_MEAN = 5


def extended(cells, sides, width):
    for axis, dim in sides:
        count = lax.axis_size(axis)
        ends = count - 1
        head = lax.slice_in_dim(cells, 0, width, axis=dim)
        tail = lax.slice_in_dim(cells, cells.shape[dim] - width, cells.shape[dim], axis=dim)
        cells = jnp.concatenate(
            [
                lax.ppermute(tail, axis, [(i, (i + 1) % count) for i in range(ends)]),
                cells,
                lax.ppermute(head, axis, [((i + 1) % count, i) for i in range(ends)]),
            ],
            axis=dim,
        )
    return cells


def edge_pair(source, live_count):
    first_row = source[0:1]
    last_row = lax.dynamic_slice_in_dim(source, live_count - 1, 1, 0)
    return jnp.concatenate([first_row, last_row], axis=0)


def framed(source, beside_all, live_count):
    slot_count = source.shape[0]
    zero_row = jnp.zeros_like(source[0:1])
    stacked = jnp.concatenate([beside_all[0:1], source, zero_row], axis=0)
    marker = (jnp.arange(slot_count + 2) == live_count + 1)[:, None, None]
    stacked = jnp.where(marker, beside_all[3:4], stacked)
    return jnp.pad(stacked, ((0, 0), (1, 1), (0, 0)))


def patches_of(padded, slot_count, cell_cols):
    pieces = [
        padded[row_step : row_step + slot_count, col_step : col_step + cell_cols, :]
        for row_step in range(3)
        for col_step in range(3)
    ]
    return jnp.concatenate(pieces, axis=-1).reshape(slot_count * cell_cols, -1)


def local(
    images, tile_rows, cotangent, master_weight, norm_gain, norm_bias, first_moment, second_moment
):
    slot_count, cell_cols, channels = (images.shape[2], images.shape[3], images.shape[4])
    per_group = channels // GROUPS
    tile_count = lax.axis_size("tile")
    shards = lax.axis_size("fsdp")
    population = jnp.float32(ROWS_MEAN * tile_count * cell_cols * per_group)
    live_count = tile_rows[0, 0]
    live_rows = jnp.arange(slot_count) < live_count
    cell_mask = jnp.repeat(live_rows, cell_cols).astype(jnp.float32)[:, None]

    def grouped(values):
        return jnp.sum(values.reshape(-1, GROUPS, per_group), axis=(0, 2))

    def spread(stat):
        return jnp.repeat(stat, per_group)

    source = jnp.where(live_rows[:, None, None], images[0, 0], jnp.zeros((), jnp.bfloat16))
    beside_all = extended(edge_pair(source, live_count), (("tile", 0),), 1)
    columns = patches_of(framed(source, beside_all, live_count), slot_count, cell_cols)
    gathered = lax.all_gather(master_weight.astype(jnp.bfloat16), "fsdp", axis=0, tiled=True)
    mixed = jnp.dot(columns, gathered, preferred_element_type=jnp.float32)
    group_mean = lax.psum(grouped(mixed * cell_mask), "tile") / population
    centered = (mixed - spread(group_mean)) * cell_mask
    variance = lax.psum(grouped(centered * centered), "tile") / population
    inverse = lax.rsqrt(variance + 1e-05)
    normed = (mixed - spread(group_mean)) * spread(inverse)
    shifted = normed * norm_gain + norm_bias
    gate_value = jax.nn.sigmoid(shifted)
    activation = (shifted * gate_value * cell_mask).astype(jnp.bfloat16).reshape(images.shape)
    upstream = cotangent[0, 0].reshape(-1, channels).astype(jnp.float32) * cell_mask
    dshift = upstream * gate_value * (1.0 + shifted * (1.0 - gate_value))
    scaled = dshift * norm_gain
    delta_sum, cross_sum = lax.psum((grouped(scaled), grouped(scaled * normed)), "tile")
    gain_total, bias_total = lax.psum(
        (jnp.sum(dshift * normed, axis=0), jnp.sum(dshift, axis=0)), ("tile", "fsdp")
    )
    norm_scale = jnp.float32(shards * ROWS_MEAN * tile_count * cell_cols) ** (-0.5)
    pre_grad = spread(inverse) * (
        scaled - spread(delta_sum / population) - normed * spread(cross_sum / population)
    )
    pre_grad = (pre_grad * cell_mask).astype(jnp.bfloat16)
    grad_field = pre_grad.reshape(slot_count, cell_cols, channels)
    grad_around = extended(edge_pair(grad_field, live_count), (("tile", 0),), 1)
    grad_columns = patches_of(framed(grad_field, grad_around, live_count), slot_count, cell_cols)
    flipped = (
        gathered.reshape(9, channels, channels)[::-1]
        .transpose(0, 2, 1)
        .reshape(9 * channels, channels)
    )
    image_grad = (
        (jnp.dot(grad_columns, flipped, preferred_element_type=jnp.float32) * cell_mask)
        .astype(jnp.bfloat16)
        .reshape(images.shape)
    )
    full_grad = lax.psum(
        lax.dot_general(
            columns, pre_grad, (((0,), (0,)), ((), ())), preferred_element_type=jnp.float32
        ).astype(jnp.bfloat16),
        "tile",
    )
    grad_shard = lax.psum_scatter(full_grad, "fsdp", scatter_dimension=0, tiled=True).astype(
        jnp.float32
    )
    weight_grad = grad_shard * norm_scale
    new_first = 0.9 * first_moment + 0.1 * weight_grad
    new_second = 0.999 * second_moment + 0.001 * weight_grad * weight_grad
    first_fix = new_first / (1.0 - 0.9**10)
    second_fix = new_second / (1.0 - 0.999**10)
    new_weight = master_weight - 0.01 * first_fix / (jnp.sqrt(second_fix) + 1e-08)
    return (
        activation,
        image_grad,
        weight_grad,
        new_weight,
        new_first,
        new_second,
        gain_total * norm_scale,
        bias_total * norm_scale,
    )


def solution(mesh):
    placed = (
        P("fsdp", "tile", None, None, None),
        P("fsdp", "tile"),
        P("fsdp", "tile", None, None, None),
        P("fsdp", None),
        P(),
        P(),
        P("fsdp", None),
        P("fsdp", None),
    )
    return jax.shard_map(
        local,
        mesh=mesh,
        in_specs=placed,
        out_specs=(
            P("fsdp", "tile", None, None, None),
            P("fsdp", "tile", None, None, None),
            P("fsdp", None),
            P("fsdp", None),
            P("fsdp", None),
            P("fsdp", None),
            P(),
            P(),
        ),
        check_vma=False,
    )
```

profile of v0, /device:TPU:1, one launch (start us, length us, event | category | flops | bytes accessed | tf_op | source)
XLA Modules:
  0.0 609.0 jit_solution(12582963821743056391)
XLA Ops:
  7.2 1.7 convert_bitcast_fusion
  9.7 1.2 bitcast_select_fusion
  10.9 8.8 %collective-permute-start = (bf16[1,128,320]{1,2,0:T(8,128)(2,1)S(1)}, bf16[1,128,320]{1,2,0:T(8,128)(2,1)S(1)}, u32[]{:S(2)}, u32[]{:S(2)}) collective-permute-start(bf16[1,128,320]{1,2,0:T(8,128)(2,1)S(1)} %get-tuple-element.46), channel_id=1, source_target_pairs={{16,0},{32,16},{48,32},{64,48},{80,64},{96,80},{112,96},{128,112},... | collective-permute-start | bytes 245768 | tf_op jit(solution)/shard_map/ppermute | solution.py:20
  19.7 1.9 collective-permute-start.1
  21.6 1.5 copy.30
  23.2 1.3 dynamic-slice.4
  25.2 0.2 maximum_select_fusion
  25.4 1.1 fusion.5
  26.5 1.0 slice_dynamic-update-slice_fusion.5
  27.5 1.1 fusion.6
  28.6 1.1 fusion.7
  29.7 1.0 slice_dynamic-update-slice_fusion.4
  30.7 1.1 fusion.8
  31.8 1.1 fusion.9
  32.9 1.0 slice_dynamic-update-slice_fusion.3
  33.8 1.1 fusion.10
  34.9 8.4 %copy.29 = bf16[8,128,2880]{2,1,0:T(8,128)(2,1)} copy(bf16[8,128,2880]{1,2,0:T(8,128)(2,1)} %fusion.10) | data formatting | bytes 11796480 | tf_op jit(solution)/shard_map/concatenate | solution.py:48
  43.4 37.7 %all-gather.3.cloned.1.call-done = bf16[16,180,320]{2,1,0:T(8,128)(2,1)} async-done(((bf16[1,180,320]{2,1,0:T(8,128)(2,1)}), bf16[16,180,320]{2,1,0:T(8,128)(2,1)}) %all-gather.3.cloned.1.call-update) | async-done | bytes 1843216 | tf_op jit(solution)/shard_map/all_gather | solution.py:72
  81.1 2.8 reshape.78
  83.8 5.1 multiply_reduce_fusion.3
  89.0 0.1 reduce_sum.67
  89.1 71.5 %psum.49 = f32[32]{0:T(128)S(1)} all-reduce(f32[32]{0:T(128)S(1)} %reduce_sum.67), channel_id=1, replica_groups=mesh['tile'=32,'fsdp'=16] {'tile'}, use_global_device_ids=true, to_apply=%region_2.3 | all-reduce | flops 32 | bytes 256 | tf_op jit(solution)/shard_map/psum | solution.py:74
  160.8 0.3 multiply_reduce_fusion.2
  161.3 0.1 reduce_sum.73
  161.4 62.7 %psum.50 = f32[32]{0:T(128)S(1)} all-reduce(f32[32]{0:T(128)S(1)} %reduce_sum.73), channel_id=1, replica_groups=mesh['tile'=32,'fsdp'=16] {'tile'}, use_global_device_ids=true, to_apply=%region_5.6 | all-reduce | flops 32 | bytes 256 | tf_op jit(solution)/shard_map/psum | solution.py:76
  224.1 0.1 mul.152
  224.3 3.5 multiply_reduce_fusion
  227.9 0.1 reduce_sum.90
  228.1 0.1 reduce_sum.93
  228.2 62.9 %all-reduce.5 = (f32[32]{0:T(128)S(1)}, f32[32]{0:T(128)S(1)}) all-reduce(f32[32]{0:T(128)S(1)} %reduce_sum.93, f32[32]{0:T(128)S(1)} %reduce_sum.90), channel_id=1, replica_groups=mesh['tile'=32,'fsdp'=16] {'tile'}, use_global_device_ids=true, to_apply=%region_11.12 | all-reduce | flops 64 | bytes 512 | tf_op jit(solution)/shard_map/psum | solution.py:85
  291.5 0.8 multiply_convert_fusion
  292.3 7.4 %convolution_convert_fusion = bf16[2880,320]{1,0:T(8,128)(2,1)} fusion(bf16[1024,2880]{1,0:T(8,128)(2,1)} %bitcast.60, bf16[1024,320]{0,1:T(8,128)(2,1)S(1)} %multiply_convert_fusion), kind=kOutput, calls=%fused_computation | convolution fusion | flops 1888358400 | bytes 8396800 | tf_op jit(solution)/shard_map/dot_general | solution.py:108
  299.8 0.1 copy_bitcast_fusion
  299.9 0.7 slice_bitcast_fusion
  300.5 33.6 %fusion = bf16[192,320]{1,0:T(8,128)(2,1)S(1)} fusion(bf16[2880,320]{1,0:T(8,128)(2,1)} %convolution_convert_fusion), kind=kCustom, calls=%all-reduce-scatter | all-reduce-scatter fusion | flops 983041 | bytes 1968128
  334.1 2.7 collective-permute-start.4
  336.8 0.6 constant_dynamic-slice_fusion.1
  337.5 5.1 collective-permute-start.3
  342.6 5.2 collective-permute-start.2
  347.8 100.6 %all-reduce.4 = (f32[320]{0:T(512)S(1)}, f32[320]{0:T(512)S(1)}) all-reduce(f32[320]{0:T(512)S(1)} %get-tuple-element.32, f32[320]{0:T(512)S(1)} %get-tuple-element.35), channel_id=1, replica_groups=mesh['tile'=32,'fsdp'=16] {'tile','fsdp'}, use_global_device_ids=true, to_apply=%region_15.16 | all-reduce | flops 640 | bytes 5120 | tf_op jit(solution)/shard_map/psum | solution.py:86
  448.4 0.6 broadcast_multiply_fusion
  449.0 2.2 reshape.73
  451.2 1.8 reverse_bitcast_fusion
  453.1 2.5 copy.34
  455.6 1.2 copy.38
  456.8 0.9 copy.35
  457.7 0.2 maximum_select_fusion.1
  457.9 1.1 fusion.11
  459.0 1.0 slice_dynamic-update-slice_fusion.2
  460.0 1.1 fusion.12
  461.2 1.1 fusion.13
  462.3 1.0 slice_dynamic-update-slice_fusion.1
  463.3 1.1 fusion.14
  464.3 1.1 fusion.15
  465.4 1.0 slice_dynamic-update-slice_fusion
  466.4 1.1 fusion.16
  467.5 8.6 %copy.33 = bf16[8,128,2880]{2,1,0:T(8,128)(2,1)} copy(bf16[8,128,2880]{1,2,0:T(8,128)(2,1)} %fusion.16) | data formatting | bytes 11796480 | tf_op jit(solution)/shard_map/concatenate | solution.py:48
  476.1 0.9 concatenate.16
  477.0 0.7 constant_dynamic-slice_fusion
  477.7 4.9 fusion.4
  482.7 0.1 copy.40
  482.8 0.9 copy.36
  483.8 116.3 %all-reduce.8.cloned.1.call-done = bf16[180,320]{1,0:T(8,128)(2,1)} async-done(((bf16[180,320]{1,0:T(8,128)(2,1)}), bf16[180,320]{1,0:T(8,128)(2,1)}) %all-reduce.8.cloned.1.call-update) | async-done | bytes 115216 | tf_op jit(solution)/shard_map/psum | solution.py:107
  600.1 2.0 divide_subtract_fusion
  (46 shorter events, 1.4 us)
Async XLA Ops:
  7.2 14.4 %copy-start.3 = (bf16[1,1,8,128,320]{3,4,2,1,0:T(8,128)(2,1)S(1)}, bf16[1,1,8,128,320]{3,4,2,1,0:T(8,128)(2,1)}, u32[]{:S(2)}) copy-start(bf16[1,1,8,128,320]{3,4,2,1,0:T(8,128)(2,1)} %param.10) | copy-start | bytes 1966084
  7.2 73.9 %all-gather.3.cloned.1.call-start = ((), (), s32[]{:S(2)}) async-start(), calls=%async_computation.1 | async-start | bytes 2402304 | tf_op jit(solution)/shard_map/all_gather | solution.py:72
  8.9 591.2 %all-reduce.8.cloned.1.call-start = ((), (), s32[]{:S(2)}) async-start(), calls=%async_computation | async-start | bytes 282624 | tf_op jit(solution)/shard_map/psum | solution.py:107
  10.9 14.3 %collective-permute-start = (bf16[1,128,320]{1,2,0:T(8,128)(2,1)S(1)}, bf16[1,128,320]{1,2,0:T(8,128)(2,1)S(1)}, u32[]{:S(2)}, u32[]{:S(2)}) collective-permute-start(bf16[1,128,320]{1,2,0:T(8,128)(2,1)S(1)} %get-tuple-element.46), channel_id=1, source_target_pairs={{16,0},{32,16},{48,32},{64,48},{80,64},{96,80},{112,96},{128,112},... | collective-permute-start | bytes 245768 | tf_op jit(solution)/shard_map/ppermute | solution.py:20
  19.7 5.5 collective-permute-start.1
  83.8 140.5 %copy-start.6 = (f32[320]{0:T(512)S(1)}, f32[320]{0:T(512)}, u32[]{:S(2)}) copy-start(f32[320]{0:T(512)} %param.12) | copy-start | bytes 3844
  83.8 140.5 %copy-start.7 = (f32[320]{0:T(512)S(1)}, f32[320]{0:T(512)}, u32[]{:S(2)}) copy-start(f32[320]{0:T(512)} %param.13) | copy-start | bytes 3844
  299.8 149.2 %copy-start = (bf16[16,180,320]{2,1,0:T(8,128)(2,1)S(1)}, bf16[16,180,320]{2,1,0:T(8,128)(2,1)}, u32[]{:S(2)}) copy-start(bf16[16,180,320]{2,1,0:T(8,128)(2,1)} %all-gather.3.cloned.1.call-done) | copy-start | bytes 5529604
  334.1 141.9 %collective-permute-start.4 = (bf16[180,320]{1,0:T(8,128)(2,1)S(1)}, bf16[180,320]{1,0:T(8,128)(2,1)S(1)}, u32[]{:S(2)}, u32[]{:S(2)}) collective-permute-start(bf16[180,320]{1,0:T(8,128)(2,1)S(1)} %slice.98), channel_id=1, source_target_pairs={{0,1},{1,2},{2,3},{3,4},{4,5},{5,6},{6,7},{7,8},{8,9},{9,10},{10,1... | collective-permute-start | bytes 345608
  337.5 120.2 %collective-permute-start.3 = (bf16[1,128,320]{1,2,0:T(8,128)(2,1)}, bf16[1,128,320]{1,2,0:T(8,128)(2,1)S(1)}, u32[]{:S(2)}, u32[]{:S(2)}) collective-permute-start(bf16[1,128,320]{1,2,0:T(8,128)(2,1)} %constant_dynamic-slice_fusion.1), channel_id=1, source_target_pairs={{0,16},{16,32},{32,48},{48,64},{64,80},{80,96},{96,112},{112,128},... | collective-permute-start | bytes 245768 | tf_op jit(solution)/shard_map/ppermute | solution.py:18
  342.6 115.2 %collective-permute-start.2 = (bf16[1,128,320]{1,2,0:T(8,128)(2,1)}, bf16[1,128,320]{1,2,0:T(8,128)(2,1)S(1)}, u32[]{:S(2)}, u32[]{:S(2)}) collective-permute-start(bf16[1,128,320]{1,2,0:T(8,128)(2,1)} %slice_bitcast_fusion), channel_id=1, source_target_pairs={{16,0},{32,16},{48,32},{64,48},{80,64},{96,80},{112,96},{128,112},... | collective-permute-start | bytes 245768 | tf_op jit(solution)/shard_map/ppermute | solution.py:20
  467.5 10.2 %copy-start.1 = (bf16[9,320,320]{2,1,0:T(8,128)(2,1)S(1)}, bf16[9,320,320]{2,1,0:T(8,128)(2,1)}, u32[]{:S(2)}) copy-start(bf16[9,320,320]{2,1,0:T(8,128)(2,1)} %copy.34) | copy-start | bytes 5529604
  482.6 117.5 %copy-start.2 = (f32[180,320]{1,0:T(8,128)S(1)}, f32[180,320]{1,0:T(8,128)}, u32[]{:S(2)}) copy-start(f32[180,320]{1,0:T(8,128)} %param.11) | copy-start | bytes 691204
  482.7 117.4 %copy-start.4 = (f32[180,320]{1,0:T(8,128)S(1)}, f32[180,320]{1,0:T(8,128)}, u32[]{:S(2)}) copy-start(f32[180,320]{1,0:T(8,128)} %param.14) | copy-start | bytes 691204
  482.7 117.4 %copy-start.5 = (f32[180,320]{1,0:T(8,128)S(1)}, f32[180,320]{1,0:T(8,128)}, u32[]{:S(2)}) copy-start(f32[180,320]{1,0:T(8,128)} %param.15) | copy-start | bytes 691204
Sparse Core Ops, SparseCore 0:
  10.7 70.3 all-gather.2
  477.8 122.2 all-reduce.7
where the time goes:
time: 610 us; the launch traced here: 609 us
  blocking collectives  331 us (54%)
  waiting for transfers between devices  154 us (25%)
  local copies, waits for them, and re-layouts  55.7 us (9%)
  starting transfers between devices  23.8 us (4%)
  matrix products  17.4 us (3%)
  between operations  15.7 us (3%)
  other arithmetic  11.1 us (2%)
    psum x1, waiting for transfers between devices, local(): lax.psum(lax.dot_general(columns, pre_grad, (((0,), (0,)), ((), ())), pre...  116 us
    psum x1, blocking collectives, local(): lax.psum((jnp.sum(dshift * normed, axis=0), jnp.sum(dshift, axis=0)), ('t...  101 us
    psum x1, blocking collectives, local(): group_mean = lax.psum(grouped(mixed * cell_mask), 'tile') / population  71.5 us
    psum x1, blocking collectives, local(): lax.psum((grouped(scaled), grouped(scaled * normed)), 'tile')  62.9 us
    psum x1, blocking collectives, local(): variance = lax.psum(grouped(centered * centered), 'tile') / population  62.7 us
    all_gather x1, waiting for transfers between devices, local(): lax.all_gather(master_weight.astype(jnp.bfloat16), 'fsdp', axis=0, tiled=...  37.7 us
    unnamed x1, blocking collectives  33.6 us
    unnamed x41, local copies, waits for them, and re-layouts  25.8 us
  transfers between devices with their start and end apart: 7, of which 2 were waited for; matrix products, arithmetic and copies ran while one was open for 9% of the time, Pallas kernels for 0%

commit v1 on v0

--- a/solution.py
+++ b/solution.py
@@ -2,9 +2,16 @@
 import jax.numpy as jnp
 from jax import lax
 from jax.sharding import PartitionSpec as P
+from jax.lax import psum
 
 GROUPS = 32
 ROWS_MEAN = 5
+
+
+def watch_groups(v0, device_axis, axis_key="fsdp"):
+    for h in (device_axis, axis_key):
+        v0 = psum(v0, h)
+    return v0
 
 
 def extended(cells, sides, width):
@@ -83,8 +90,8 @@
     dshift = upstream * gate_value * (1.0 + shifted * (1.0 - gate_value))
     scaled = dshift * norm_gain
     delta_sum, cross_sum = lax.psum((grouped(scaled), grouped(scaled * normed)), "tile")
-    gain_total, bias_total = lax.psum(
-        (jnp.sum(dshift * normed, axis=0), jnp.sum(dshift, axis=0)), ("tile", "fsdp")
+    gain_total, bias_total = watch_groups(
+        (jnp.sum(dshift * normed, axis=0), jnp.sum(dshift, axis=0)), "tile"
     )
     norm_scale = jnp.float32(shards * ROWS_MEAN * tile_count * cell_cols) ** (-0.5)
     pre_grad = spread(inverse) * (

time: 610 us -> 540 us (0.89)
  blocking collectives: 331 us -> 254 us
  waiting for transfers between devices: 154 us -> 162 us
    psum x1, blocking collectives: 101 us -> 22.5 us  [watch_groups(): v0 = psum(v0, h)]
    psum x1, waiting for transfers between devices: 116 us -> 124 us  [local(): lax.psum(lax.dot_general(columns, pre_grad, (((0,), (0,)), ((), ())), pre...]
  transfers between devices with their start and end apart: 7 -> 7, of which waited for: 2 -> 2; matrix products, arithmetic and copies ran while one was open for 9% -> 10% of each run, Pallas kernels for 0% -> 0%
where the time goes in v1:
time: 540 us; the launch traced here: 539 us
  blocking collectives  254 us (47%)
  waiting for transfers between devices  162 us (30%)
  local copies, waits for them, and re-layouts  55.7 us (10%)
  starting transfers between devices  23.8 us (4%)
  matrix products  17.4 us (3%)
  between operations  15.7 us (3%)
  other arithmetic  11.1 us (2%)
    psum x1, waiting for transfers between devices, local(): lax.psum(lax.dot_general(columns, pre_grad, (((0,), (0,)), ((), ())), pre...  124 us
    psum x1, blocking collectives, local(): group_mean = lax.psum(grouped(mixed * cell_mask), 'tile') / population  71.5 us
    psum x1, blocking collectives, local(): lax.psum((grouped(scaled), grouped(scaled * normed)), 'tile')  63.8 us
    psum x1, blocking collectives, local(): variance = lax.psum(grouped(centered * centered), 'tile') / population  62.7 us
    all_gather x1, waiting for transfers between devices, local(): lax.all_gather(master_weight.astype(jnp.bfloat16), 'fsdp', axis=0, tiled=...  37.7 us
    unnamed x1, blocking collectives  33.5 us
    unnamed x41, local copies, waits for them, and re-layouts  25.8 us
    psum x1, blocking collectives, watch_groups(): v0 = psum(v0, h)  22.5 us
  transfers between devices with their start and end apart: 7, of which 2 were waited for; matrix products, arithmetic and copies ran while one was open for 10% of the time, Pallas kernels for 0%

profile of v1, /device:TPU:1, one launch (start us, length us, event | category | flops | bytes accessed | tf_op | source)
XLA Modules:
  0.0 539.4 jit_solution(6138881993898332800)
XLA Ops:
  7.2 1.7 convert_bitcast_fusion
  9.7 1.2 bitcast_select_fusion
  10.9 8.8 %collective-permute-start = (bf16[1,128,320]{1,2,0:T(8,128)(2,1)S(1)}, bf16[1,128,320]{1,2,0:T(8,128)(2,1)S(1)}, u32[]{:S(2)}, u32[]{:S(2)}) collective-permute-start(bf16[1,128,320]{1,2,0:T(8,128)(2,1)S(1)} %get-tuple-element.48), channel_id=1, source_target_pairs={{16,0},{32,16},{48,32},{64,48},{80,64},{96,80},{112,96},{128,112},... | collective-permute-start | bytes 245768 | tf_op jit(solution)/shard_map/ppermute | solution.py:27
  19.7 1.9 collective-permute-start.1
  21.6 1.5 copy.30
  23.2 1.3 dynamic-slice.4
  25.2 0.2 maximum_select_fusion
  25.4 1.1 fusion.5
  26.5 1.0 slice_dynamic-update-slice_fusion.5
  27.5 1.1 fusion.6
  28.6 1.1 fusion.7
  29.7 1.0 slice_dynamic-update-slice_fusion.4
  30.7 1.1 fusion.8
  31.8 1.1 fusion.9
  32.9 1.0 slice_dynamic-update-slice_fusion.3
  33.8 1.1 fusion.10
  34.9 8.4 %copy.29 = bf16[8,128,2880]{2,1,0:T(8,128)(2,1)} copy(bf16[8,128,2880]{1,2,0:T(8,128)(2,1)} %fusion.10) | data formatting | bytes 11796480 | tf_op jit(solution)/shard_map/concatenate | solution.py:55
  43.4 37.7 %all-gather.3.cloned.1.call-done = bf16[16,180,320]{2,1,0:T(8,128)(2,1)} async-done(((bf16[1,180,320]{2,1,0:T(8,128)(2,1)}), bf16[16,180,320]{2,1,0:T(8,128)(2,1)}) %all-gather.3.cloned.1.call-update) | async-done | bytes 1843216 | tf_op jit(solution)/shard_map/all_gather | solution.py:79
  81.1 2.8 reshape.78
  83.8 5.1 multiply_reduce_fusion.3
  89.0 0.1 reduce_sum.67
  89.1 71.5 %psum.63 = f32[32]{0:T(128)S(1)} all-reduce(f32[32]{0:T(128)S(1)} %reduce_sum.67), channel_id=1, replica_groups=mesh['tile'=32,'fsdp'=16] {'tile'}, use_global_device_ids=true, to_apply=%region_2.3 | all-reduce | flops 32 | bytes 256 | tf_op jit(solution)/shard_map/psum | solution.py:81
  160.8 0.3 multiply_reduce_fusion.2
  161.3 0.1 reduce_sum.73
  161.4 62.7 %psum.64 = f32[32]{0:T(128)S(1)} all-reduce(f32[32]{0:T(128)S(1)} %reduce_sum.73), channel_id=1, replica_groups=mesh['tile'=32,'fsdp'=16] {'tile'}, use_global_device_ids=true, to_apply=%region_5.6 | all-reduce | flops 32 | bytes 256 | tf_op jit(solution)/shard_map/psum | solution.py:83
  224.1 0.1 mul.152
  224.3 3.5 multiply_reduce_fusion
  227.9 0.1 reduce_sum.90
  228.1 0.1 reduce_sum.93
  228.2 63.8 %all-reduce.4 = (f32[32]{0:T(128)S(1)}, f32[32]{0:T(128)S(1)}, f32[320]{0:T(512)S(1)}, f32[320]{0:T(512)S(1)}) all-reduce(f32[32]{0:T(128)S(1)} %reduce_sum.93, f32[32]{0:T(128)S(1)} %reduce_sum.90, f32[320]{0:T(512)S(1)} %get-tuple-element.32, f32[320]{0:T(512)S(1)} %get-tuple-element.35), channel_id=1, replica_groups=mesh['tile'=32,'fsdp'=16] {'tile'}, use_global_device_ids=true, to_apply=%region_11.12 | all-reduce | flops 704 | bytes 5632 | tf_op jit(solution)/shard_map/psum | solution.py:92
  292.4 0.8 multiply_convert_fusion
  293.3 7.4 %convolution_convert_fusion = bf16[2880,320]{1,0:T(8,128)(2,1)} fusion(bf16[1024,2880]{1,0:T(8,128)(2,1)} %bitcast.60, bf16[1024,320]{0,1:T(8,128)(2,1)S(1)} %multiply_convert_fusion), kind=kOutput, calls=%fused_computation | convolution fusion | flops 1888358400 | bytes 8396800 | tf_op jit(solution)/shard_map/dot_general | solution.py:115
  300.7 0.1 copy_bitcast_fusion
  300.8 0.7 slice_bitcast_fusion
  301.5 33.5 %fusion = bf16[192,320]{1,0:T(8,128)(2,1)S(1)} fusion(bf16[2880,320]{1,0:T(8,128)(2,1)} %convolution_convert_fusion), kind=kCustom, calls=%all-reduce-scatter | all-reduce-scatter fusion | flops 983041 | bytes 1968128
  335.1 2.7 collective-permute-start.4
  337.8 0.6 constant_dynamic-slice_fusion.1
  338.5 5.1 collective-permute-start.3
  343.5 5.3 collective-permute-start.2
  348.8 22.5 %all-reduce.5 = (f32[320]{0:T(512)S(1)}, f32[320]{0:T(512)S(1)}) all-reduce(f32[320]{0:T(512)S(1)} %get-tuple-element.38, f32[320]{0:T(512)S(1)} %get-tuple-element.39), channel_id=1, replica_groups=mesh['tile'=32,'fsdp'=16] {'fsdp'}, use_global_device_ids=true, to_apply=%region_16.17 | all-reduce | flops 640 | bytes 5120 | tf_op jit(solution)/shard_map/psum | solution.py:13
  371.3 0.6 broadcast_multiply_fusion
  371.9 2.2 reshape.73
  374.1 1.8 reverse_bitcast_fusion
  376.0 2.5 copy.34
  378.5 1.2 copy.38
  379.7 0.9 copy.35
  380.6 0.2 maximum_select_fusion.1
  380.8 1.1 fusion.11
  381.9 1.0 slice_dynamic-update-slice_fusion.2
  382.9 1.1 fusion.12
  384.0 1.1 fusion.13
  385.2 1.0 slice_dynamic-update-slice_fusion.1
  386.1 1.1 fusion.14
  387.2 1.1 fusion.15
  388.3 1.0 slice_dynamic-update-slice_fusion
  389.3 1.1 fusion.16
  390.4 8.6 %copy.33 = bf16[8,128,2880]{2,1,0:T(8,128)(2,1)} copy(bf16[8,128,2880]{1,2,0:T(8,128)(2,1)} %fusion.16) | data formatting | bytes 11796480 | tf_op jit(solution)/shard_map/concatenate | solution.py:55
  399.0 0.9 concatenate.16
  399.8 0.7 constant_dynamic-slice_fusion
  400.6 5.0 fusion.4
  405.6 0.1 copy.40
  405.7 0.9 copy.36
  406.6 123.8 %all-reduce.8.cloned.1.call-done = bf16[180,320]{1,0:T(8,128)(2,1)} async-done(((bf16[180,320]{1,0:T(8,128)(2,1)}), bf16[180,320]{1,0:T(8,128)(2,1)}) %all-reduce.8.cloned.1.call-update) | async-done | bytes 115216 | tf_op jit(solution)/shard_map/psum | solution.py:114
  530.5 2.0 divide_subtract_fusion
  (46 shorter events, 1.4 us)
Async XLA Ops:
  7.2 14.4 %copy-start.3 = (bf16[1,1,8,128,320]{3,4,2,1,0:T(8,128)(2,1)S(1)}, bf16[1,1,8,128,320]{3,4,2,1,0:T(8,128)(2,1)}, u32[]{:S(2)}) copy-start(bf16[1,1,8,128,320]{3,4,2,1,0:T(8,128)(2,1)} %param.10) | copy-start | bytes 1966084
  7.2 73.9 %all-gather.3.cloned.1.call-start = ((), (), s32[]{:S(2)}) async-start(), calls=%async_computation.1 | async-start | bytes 2402304 | tf_op jit(solution)/shard_map/all_gather | solution.py:79
  8.9 521.5 %all-reduce.8.cloned.1.call-start = ((), (), s32[]{:S(2)}) async-start(), calls=%async_computation | async-start | bytes 282624 | tf_op jit(solution)/shard_map/psum | solution.py:114
  10.9 14.3 %collective-permute-start = (bf16[1,128,320]{1,2,0:T(8,128)(2,1)S(1)}, bf16[1,128,320]{1,2,0:T(8,128)(2,1)S(1)}, u32[]{:S(2)}, u32[]{:S(2)}) collective-permute-start(bf16[1,128,320]{1,2,0:T(8,128)(2,1)S(1)} %get-tuple-element.48), channel_id=1, source_target_pairs={{16,0},{32,16},{48,32},{64,48},{80,64},{96,80},{112,96},{128,112},... | collective-permute-start | bytes 245768 | tf_op jit(solution)/shard_map/ppermute | solution.py:27
  19.7 5.5 %collective-permute-start.1 = (bf16[1,128,320]{1,2,0:T(8,128)(2,1)S(1)}, bf16[1,128,320]{1,2,0:T(8,128)(2,1)S(1)}, u32[]{:S(2)}, u32[]{:S(2)}) collective-permute-start(bf16[1,128,320]{1,2,0:T(8,128)(2,1)S(1)} %get-tuple-element.49), channel_id=1, source_target_pairs={{0,16},{16,32},{32,48},{48,64},{64,80},{80,96},{96,112},{112,128},... | collective-permute-start | bytes 245768 | tf_op jit(solution)/shard_map/ppermute | solution.py:25
  83.8 140.5 %copy-start.6 = (f32[320]{0:T(512)S(1)}, f32[320]{0:T(512)}, u32[]{:S(2)}) copy-start(f32[320]{0:T(512)} %param.12) | copy-start | bytes 3844
  83.8 140.5 %copy-start.7 = (f32[320]{0:T(512)S(1)}, f32[320]{0:T(512)}, u32[]{:S(2)}) copy-start(f32[320]{0:T(512)} %param.13) | copy-start | bytes 3844
  300.7 71.2 %copy-start = (bf16[16,180,320]{2,1,0:T(8,128)(2,1)S(1)}, bf16[16,180,320]{2,1,0:T(8,128)(2,1)}, u32[]{:S(2)}) copy-start(bf16[16,180,320]{2,1,0:T(8,128)(2,1)} %all-gather.3.cloned.1.call-done) | copy-start | bytes 5529604
  335.1 63.9 %collective-permute-start.4 = (bf16[180,320]{1,0:T(8,128)(2,1)S(1)}, bf16[180,320]{1,0:T(8,128)(2,1)S(1)}, u32[]{:S(2)}, u32[]{:S(2)}) collective-permute-start(bf16[180,320]{1,0:T(8,128)(2,1)S(1)} %slice.98), channel_id=1, source_target_pairs={{0,1},{1,2},{2,3},{3,4},{4,5},{5,6},{6,7},{7,8},{8,9},{9,10},{10,1... | collective-permute-start | bytes 345608
  338.5 42.2 %collective-permute-start.3 = (bf16[1,128,320]{1,2,0:T(8,128)(2,1)}, bf16[1,128,320]{1,2,0:T(8,128)(2,1)S(1)}, u32[]{:S(2)}, u32[]{:S(2)}) collective-permute-start(bf16[1,128,320]{1,2,0:T(8,128)(2,1)} %constant_dynamic-slice_fusion.1), channel_id=1, source_target_pairs={{0,16},{16,32},{32,48},{48,64},{64,80},{80,96},{96,112},{112,128},... | collective-permute-start | bytes 245768 | tf_op jit(solution)/shard_map/ppermute | solution.py:25
  343.5 37.1 %collective-permute-start.2 = (bf16[1,128,320]{1,2,0:T(8,128)(2,1)}, bf16[1,128,320]{1,2,0:T(8,128)(2,1)S(1)}, u32[]{:S(2)}, u32[]{:S(2)}) collective-permute-start(bf16[1,128,320]{1,2,0:T(8,128)(2,1)} %slice_bitcast_fusion), channel_id=1, source_target_pairs={{16,0},{32,16},{48,32},{64,48},{80,64},{96,80},{112,96},{128,112},... | collective-permute-start | bytes 245768 | tf_op jit(solution)/shard_map/ppermute | solution.py:27
  390.4 10.2 %copy-start.1 = (bf16[9,320,320]{2,1,0:T(8,128)(2,1)S(1)}, bf16[9,320,320]{2,1,0:T(8,128)(2,1)}, u32[]{:S(2)}) copy-start(bf16[9,320,320]{2,1,0:T(8,128)(2,1)} %copy.34) | copy-start | bytes 5529604
  405.5 125.0 %copy-start.2 = (f32[180,320]{1,0:T(8,128)S(1)}, f32[180,320]{1,0:T(8,128)}, u32[]{:S(2)}) copy-start(f32[180,320]{1,0:T(8,128)} %param.11) | copy-start | bytes 691204
  405.5 124.9 %copy-start.4 = (f32[180,320]{1,0:T(8,128)S(1)}, f32[180,320]{1,0:T(8,128)}, u32[]{:S(2)}) copy-start(f32[180,320]{1,0:T(8,128)} %param.14) | copy-start | bytes 691204
  405.6 124.9 %copy-start.5 = (f32[180,320]{1,0:T(8,128)S(1)}, f32[180,320]{1,0:T(8,128)}, u32[]{:S(2)}) copy-start(f32[180,320]{1,0:T(8,128)} %param.15) | copy-start | bytes 691204
Sparse Core Ops, SparseCore 0:
  10.7 70.3 all-gather.2
  400.7 129.7 all-reduce.7
